TPU v7x, 32 devices: a whole 2x2x4 slice. The times are simulated.
32 devices in a mesh: pts: 8 (over z, y), grp: 4 (over x, core).
Axes of the slice: x: 2, y: 2, z: 4, core: 2. Of those that a mesh axis runs over, the one named last changes fastest.
Arguments:
- jacobian: bfloat16 [32, 6, 128, 3, 256], P(('pts', 'grp')), may hold values from -0.21875 to 0.21875
- point_blocks: float32 [32, 6, 256], P(('pts', 'grp')), may hold values from -0.5 to 4, as said below
- point_grad: bfloat16 [32, 3, 256], P(('pts', 'grp')), may hold values from -6 to 6
- camera_grad: float32 [32, 128], P(('pts', 'grp')), may hold values from -6 to 6
- damping: float32 [32, 128], replicated, may hold values from 1 to 8
- incidence: int32 [32, 6], P(('pts', 'grp')), may hold values from 0 to 31, as said below
- tile_owner: int32 [8], replicated, may hold values from 0 to 7, each once
- front_first: int32 [1], replicated, may hold values from 0 to 31
Outputs:
- tiles_out: float32 [256, 128, 128], P(('pts', 'grp'))
- rhs_out: float32 [32, 128], P(('pts', 'grp'))
- front_panel: float32 [2304, 512], P(None, 'grp')
Inputs may be any that keep to these rules, and one draw needn't show every extreme that they name: `incidence`: point cluster p names 6 different camera clusters, all among (p + t) mod 32 for t from 0 to 7. `point_blocks`: each point's diagonal entries exceed the sum of the magnitudes of the two off-diagonal entries of their row by 0.1 or more. `tile_owner`: A permutation of the pts indices.
All inputs are finite; a program needn't handle non-finite values.
Results may differ from a plain program's by a relative error of at most 0.0022.
Values sent between devices are 32-bit elements; how exact they have to be, the bound alone decides.
No kernel may reach another device: no remote copies, remote signals or barrier semaphores. Data moves between devices by JAX's collectives and lax.ppermute only.
A program may use at most 128 MiB of HBM per device.

v0:
```python
import jax
import jax.numpy as jnp
import numpy as np
from jax import lax
from jax.sharding import PartitionSpec as P

TOUCH = 6
BAND = 8
FRONT = 4


PRECISE = lax.Precision.HIGHEST


def shifted(value, axis, steps):
    count = lax.axis_size(axis)
    pairs = [(source, (source + steps) % count) for source in range(count)]
    return lax.ppermute(value, axis, pairs)


def invert_blocks(blocks):
    diag_x = blocks[:, 0]
    diag_y = blocks[:, 1]
    diag_z = blocks[:, 2]
    cross_xy = blocks[:, 3]
    cross_xz = blocks[:, 4]
    cross_yz = blocks[:, 5]
    adj_xx = diag_y * diag_z - cross_yz * cross_yz
    adj_yy = diag_x * diag_z - cross_xz * cross_xz
    adj_zz = diag_x * diag_y - cross_xy * cross_xy
    adj_xy = cross_xz * cross_yz - cross_xy * diag_z
    adj_xz = cross_xy * cross_yz - diag_y * cross_xz
    adj_yz = cross_xy * cross_xz - diag_x * cross_yz
    determinant = diag_x * adj_xx + cross_xy * adj_xy + cross_xz * adj_xz
    inverse_det = 1.0 / determinant
    return [
        [adj_xx * inverse_det, adj_xy * inverse_det, adj_xz * inverse_det],
        [adj_xy * inverse_det, adj_yy * inverse_det, adj_yz * inverse_det],
        [adj_xz * inverse_det, adj_yz * inverse_det, adj_zz * inverse_det],
    ]


def scale_jacobian(jacobian, blocks):
    inverse = invert_blocks(blocks)
    widened = jacobian.astype(jnp.float32)
    columns = []
    for target in range(3):
        summed = widened[:, :, :, 0, :] * inverse[0][target][:, None, None, :]
        summed = summed + widened[:, :, :, 1, :] * inverse[1][target][:, None, None, :]
        summed = summed + widened[:, :, :, 2, :] * inverse[2][target][:, None, None, :]
        columns.append(summed)
    return jnp.stack(columns, axis=3).astype(jnp.bfloat16)


def band_table(reach_rows, reach_sum):
    row_list = []
    offset_list = []
    for row_pos in range(reach_rows):
        for offset in range(BAND):
            if row_pos + offset <= reach_sum:
                row_list.append(row_pos)
                offset_list.append(offset)
    return (np.array(row_list), np.array(offset_list))


def route_rows(tiles, tile_owner, base, row_list, offset_list, pts_count):
    offsets = BAND * row_list + offset_list
    capacity = int(offsets.max()) // pts_count + 1
    residue = jnp.mod(base + jnp.asarray(offsets), pts_count)
    target = tile_owner[residue] * capacity + jnp.asarray(offsets // pts_count)
    sending = (jnp.arange(pts_count * capacity)[:, None] == target[None, :]).astype(jnp.float32)
    return (jnp.einsum("dt,trc->drc", sending, tiles, precision=PRECISE), capacity)


def collect_rows(
    incoming, capacity, perm_inverse, anchors, usable_test, clusters, grp_count, pts_count
):
    sender = jnp.arange(pts_count * capacity) // capacity
    slot_of = jnp.arange(pts_count * capacity) % capacity
    sender_anchor = anchors(sender)
    arrived = jnp.mod(perm_inverse - BAND * sender_anchor, pts_count) + slot_of * pts_count
    row_pos = arrived // BAND
    offset = arrived % BAND
    usable = usable_test(row_pos, offset)
    home_row = jnp.mod(sender_anchor + row_pos, clusters)
    owner_slot = (BAND * home_row + offset) // pts_count
    gathering = (
        (jnp.arange(BAND * grp_count)[:, None] == owner_slot[None, :]) & usable[None, :]
    ).astype(jnp.float32)
    return jnp.einsum("ms,src->mrc", gathering, incoming, precision=PRECISE)


def per_device(
    jacobian, point_blocks, point_grad, camera_grad, damping, incidence, tile_owner, front_first
):
    pts_count = lax.axis_size("pts")
    grp_count = lax.axis_size("grp")
    clusters = pts_count * grp_count
    my_grp = lax.axis_index("grp")
    my_pts = lax.axis_index("pts")
    device = my_pts * grp_count + my_grp
    local_count = jacobian.shape[0]
    cam_rows = jacobian.shape[2]
    point_cols = 3 * jacobian.shape[4]
    window_len = 2 * BAND - 2 + FRONT
    reach = 2 * BAND - 1
    scaled = scale_jacobian(jacobian, point_blocks).reshape(
        local_count, TOUCH, cam_rows, point_cols
    )
    jac_flat = jacobian.reshape(local_count, TOUCH, cam_rows, point_cols)
    local_slot = jnp.mod(incidence - device, clusters)
    placing = (local_slot[:, None, :] == jnp.arange(BAND)[None, :, None]).astype(jnp.bfloat16)
    placed_scaled = jnp.einsum(
        "ptk,pkrx->ptrx", placing, scaled, preferred_element_type=jnp.float32
    ).astype(jnp.bfloat16)
    placed_jac = jnp.einsum(
        "ptk,pkrx->ptrx", placing, jac_flat, preferred_element_type=jnp.float32
    ).astype(jnp.bfloat16)
    band_grid = jnp.einsum(
        "ptrx,pqcx->tqrc", placed_scaled, placed_jac, preferred_element_type=jnp.float32
    )
    band_rhs = jnp.einsum(
        "ptrx,px->tr",
        placed_scaled,
        point_grad.reshape(local_count, point_cols),
        preferred_element_type=jnp.float32,
    )
    perm_inverse = jnp.sum(jnp.arange(pts_count) * (tile_owner == my_pts))
    row_list, offset_list = band_table(BAND, BAND - 1)
    band_tiles = band_grid[row_list, row_list + offset_list]
    quarters = lax.all_to_all(band_tiles, "grp", split_axis=1, concat_axis=0, tiled=True)
    reach_union = BAND + grp_count - 2
    union_rows_list, union_offsets = band_table(reach_union + 1, reach_union)
    lookup = {}
    for position in range(len(union_rows_list)):
        lookup[int(union_rows_list[position]), int(union_offsets[position])] = position
    merge_table = np.zeros((len(union_rows_list), grp_count * len(row_list)), np.float32)
    for source_grp in range(grp_count):
        for position in range(len(row_list)):
            merge_table[
                lookup[source_grp + int(row_list[position]), int(offset_list[position])],
                source_grp * len(row_list) + position,
            ] = 1.0
    union_rows = jnp.einsum("us,src->urc", jnp.asarray(merge_table), quarters, precision=PRECISE)
    outgoing, capacity = route_rows(
        union_rows, tile_owner, BAND * grp_count * my_pts, union_rows_list, union_offsets, pts_count
    )
    incoming = lax.all_to_all(outgoing, "pts", split_axis=0, concat_axis=0, tiled=True)
    owner_rows = collect_rows(
        incoming,
        capacity,
        perm_inverse,
        lambda sender: sender * grp_count,
        lambda row_pos, offset: row_pos + offset <= reach_union,
        clusters,
        grp_count,
        pts_count,
    )
    owned = lax.all_to_all(owner_rows, "grp", split_axis=0, concat_axis=1, tiled=True)
    tile_id = perm_inverse + pts_count * (BAND * my_grp + jnp.arange(BAND))
    home_row = tile_id // BAND
    offset = tile_id % BAND
    other_row = jnp.mod(home_row + offset, clusters)
    pick_damp = (home_row[:, None] == jnp.arange(clusters)[None, :]).astype(jnp.float32)
    damp_rows = jnp.dot(pick_damp, damping, precision=PRECISE)
    identity = jnp.eye(cam_rows, dtype=jnp.float32)
    owned = owned + jnp.where(
        (offset == 0)[:, None, None], damp_rows[:, :, None] * identity[None, :, :], 0.0
    )
    summed = band_rhs[0]
    for step in range(1, BAND):
        summed = summed + shifted(band_rhs[step], ("pts", "grp"), step)
    reduced = camera_grad - summed[None, :]
    front_start = front_first[0]
    window_base = front_start - (BAND - 1)
    pos_home = jnp.mod(home_row - window_base, clusters)
    pos_other = jnp.mod(other_row - window_base, clusters)
    front_axis = jnp.arange(FRONT)[:, None, None]
    reach_axis = jnp.arange(reach)[None, :, None]
    direct = (
        (pos_other[None, None, :] == BAND - 1 + front_axis)
        & (pos_home[None, None, :] == front_axis + reach_axis)
    ).astype(jnp.float32)
    mirror = (
        (pos_home[None, None, :] == BAND - 1 + front_axis)
        & (offset[None, None, :] > 0)
        & (pos_other[None, None, :] == front_axis + reach_axis)
    ).astype(jnp.float32)
    front_rows = jnp.einsum("kes,sab->keab", direct, owned, precision=PRECISE) + jnp.einsum(
        "kes,sba->keab", mirror, owned, precision=PRECISE
    )
    my_pos = jnp.mod(device - window_base, clusters)
    window_rhs = (jnp.arange(window_len)[:, None] == my_pos).astype(jnp.float32) * reduced
    front_rows, window_rhs = lax.psum((front_rows, window_rhs), ("pts", "grp"))
    flat_rows = jnp.concatenate(
        [
            front_rows.reshape(FRONT * reach, cam_rows, cam_rows),
            jnp.zeros((1, cam_rows, cam_rows), jnp.float32),
        ],
        axis=0,
    )
    lookup_table = np.full((window_len, FRONT), FRONT * reach, np.int32)
    for position in range(window_len):
        for front_pos in range(FRONT):
            if 0 <= position - front_pos < reach:
                lookup_table[position, front_pos] = front_pos * reach + position - front_pos
    columns = (
        flat_rows[lookup_table]
        .transpose(0, 2, 1, 3)
        .reshape(window_len * cam_rows, FRONT * cam_rows)
    )
    square = columns[(BAND - 1) * cam_rows : (BAND - 1 + FRONT) * cam_rows]
    factor = jnp.linalg.cholesky(square)
    panel = jax.scipy.linalg.solve_triangular(factor, columns.T, lower=True).T
    share = FRONT * cam_rows // grp_count
    front_panel = lax.dynamic_slice_in_dim(panel, my_grp * share, share, 1)
    panel_blocks = panel.reshape(window_len, cam_rows, FRONT * cam_rows)

    def inside_rest(position):
        return (position < window_len) & ((position < BAND - 1) | (position >= BAND - 1 + FRONT))

    update_mask = inside_rest(pos_home) & inside_rest(pos_other)
    pick_home = (pos_home[:, None] == jnp.arange(window_len)[None, :]).astype(jnp.float32)
    pick_other = (pos_other[:, None] == jnp.arange(window_len)[None, :]).astype(jnp.float32)
    rows_home = jnp.einsum("sp,pra->sra", pick_home, panel_blocks, precision=PRECISE)
    rows_other = jnp.einsum("sp,pra->sra", pick_other, panel_blocks, precision=PRECISE)
    change = jnp.einsum("sra,sca->src", rows_home, rows_other, precision=PRECISE)
    tiles_out = owned - jnp.where(update_mask[:, None, None], change, 0.0)
    solved_front = jax.scipy.linalg.solve_triangular(
        factor, window_rhs[BAND - 1 : BAND - 1 + FRONT].reshape(FRONT * cam_rows), lower=True
    )
    my_row = lax.dynamic_index_in_dim(
        panel_blocks, jnp.clip(my_pos, 0, window_len - 1), 0, keepdims=False
    )
    correction = reduced[0] - jnp.dot(my_row, solved_front, precision=PRECISE)
    front_piece = lax.dynamic_index_in_dim(
        solved_front.reshape(FRONT, cam_rows),
        jnp.clip(my_pos - (BAND - 1), 0, FRONT - 1),
        0,
        keepdims=False,
    )
    in_front = (my_pos >= BAND - 1) & (my_pos < BAND - 1 + FRONT)
    in_window = my_pos < window_len
    rhs_out = jnp.where(in_front, front_piece, jnp.where(in_window, correction, reduced[0]))[
        None, :
    ]
    return (tiles_out, rhs_out, front_panel)


def solution(mesh):
    in_specs = (
        P(("pts", "grp"), None, None, None, None),
        P(("pts", "grp"), None, None),
        P(("pts", "grp"), None, None),
        P(("pts", "grp"), None),
        P(),
        P(("pts", "grp"), None),
        P(),
        P(),
    )
    out_specs = (P(("pts", "grp"), None, None), P(("pts", "grp"), None), P(None, "grp"))
    return jax.shard_map(
        per_device, mesh=mesh, in_specs=in_specs, out_specs=out_specs, check_vma=False
    )
```

profile of v0, /device:TPU:0, one launch (start us, length us, event | category | flops | bytes accessed | tf_op | source)
XLA Modules:
  0.0 494.4 jit_solution(7508762552952673536)
XLA Ops:
  18.5 3.5 convolution_bitcast_fusion
  27.1 4.4 all-to-all-start
  32.2 5.0 %fusion.120 = s32[60]{0:T(128)S(1)} fusion(s32[60]{0:T(128)S(1)} %copy-done.16, s32[60]{0:T(128)S(1)} %copy-done.15, s32[]{:T(128)} %bitcast.1, s32[]{:T(128)} %bitcast.2, s32[]{:T(128)} %bitcast.3, s32[]{:T(128)} %bitcast.4, s32[]{:T(128)} %bitcast.5, s32[]{:T(128)} %bitcast.6, s32[]{:T(128)} %bitcast.7, s32[]{:T(128)} %bitcast.8, s32[]{:T(128)S(6)} %mul.589), kind=kLoop, calls=%fused_computation.234 | loop fusion | flops 1860 | bytes 756 | tf_op jit(solution)/shard_map/add | solution.py:70
  37.1 25.7 %all-to-all-done = f32[36,128,128]{2,0,1:T(8,128)S(1)} async-done(((f32[36,128,128]{2,0,1:T(8,128)}), f32[36,128,128]{2,0,1:T(8,128)S(1)}, u32[]{:S(2)}, u32[]{:S(2)}) %all-to-all-start) | async-done | bytes 2359328 | tf_op jit(solution)/shard_map/all_to_all | solution.py:131
  68.2 6.6 %all-to-all-start.1 = ((f32[88,32,128]{2,1,0:T(8,128)}), f32[88,32,128]{2,1,0:T(8,128)S(1)}, u32[]{:S(2)}, u32[]{:S(2)}) async-start(f32[88,32,128]{2,1,0:T(8,128)} %copy.52), calls=%async_computation.1 | async-start | bytes 2883584 | tf_op jit(solution)/shard_map/all_to_all | solution.py:148
  78.3 30.5 %all-to-all-done.1 = f32[88,32,128]{2,1,0:T(8,128)S(1)} async-done(((f32[88,32,128]{2,1,0:T(8,128)}), f32[88,32,128]{2,1,0:T(8,128)S(1)}, u32[]{:S(2)}, u32[]{:S(2)}) %all-to-all-start.1) | async-done | bytes 1441824 | tf_op jit(solution)/shard_map/all_to_all | solution.py:148
  111.3 3.5 all-to-all-start.2
  116.0 7.6 %all-to-all-done.2 = f32[32,32,128]{2,1,0:T(8,128)S(1)} async-done(((f32[32,32,128]{2,1,0:T(8,128)}), f32[32,32,128]{2,1,0:T(8,128)S(1)}, u32[]{:S(2)}, u32[]{:S(2)}) %all-to-all-start.2) | async-done | bytes 524320 | tf_op jit(solution)/shard_map/all_to_all | solution.py:159
  128.0 3.1 copy.58
  132.5 3.5 fusion.148
  138.9 3.9 collective-permute-done
  145.4 3.7 collective-permute-done.5
  149.2 39.0 %psum.15 = f32[18,128]{1,0:T(8,128)S(1)} all-reduce(f32[18,128]{1,0:T(8,128)S(1)} %broadcast_multiply_fusion), channel_id=1, replica_groups=mesh['pts'=8,'grp'=4] {'pts','grp'}, use_global_device_ids=true, to_apply=%region_10.11 | all-reduce | flops 2304 | bytes 18432 | tf_op jit(solution)/shard_map/psum | solution.py:194
  188.2 82.6 %all-reduce.4.cloned.1.call-done = f32[60,128,128]{2,1,0:T(8,128)} async-done(((f32[60,128,128]{2,1,0:T(8,128)}), f32[60,128,128]{2,1,0:T(8,128)}) %all-reduce.4.cloned.1.call-update) | async-done | bytes 3932176 | tf_op jit(solution)/shard_map/psum | solution.py:194
  270.8 4.5 concatenate.34
  275.3 5.2 %gather_fusion.1 = f32[72,128,128]{2,1,0:T(8,128)} fusion(f32[61,128,128]{2,1,0:T(8,128)} %concatenate.34, s32[1024]{0:T(1024)S(1)} %pad_clamp_fusion), kind=kCustom, calls=%fused_computation.1 | custom fusion | bytes 9437472 | tf_op jit(solution)/shard_map/gather | solution.py:208
  286.0 11.7 %cholesky.86 = f32[128,128]{1,0:T(8,128)S(1)} custom-call(f32[128,128]{1,0:T(8,128)S(1)} %cholesky.232), custom_call_target="Cholesky" | custom-call | tf_op jit(solution)/shard_map/jit(cholesky)/cholesky | solution.py:213
  297.9 14.8 %copy.75 = f32[18,128,4,128]{1,0,3,2:T(8,128)} copy(f32[18,128,4,128]{3,1,2,0:T(8,128)} %bitcast.269) | data formatting | bytes 9437184 | tf_op jit(solution)/shard_map/reshape | solution.py:210
  312.7 9.8 %custom-call.34 = f32[1,128,128]{1,2,0:T(8,128)S(1)} custom-call(f32[1,128,128]{2,1,0:T(8,128)S(1)} %get-tuple-element.50), custom_call_target="InvertDiagBlocksLowerTriangular" | custom-call | tf_op jit(solution)/shard_map/jit(cholesky)/cholesky | solution.py:213
  323.2 11.7 %cholesky.183 = f32[128,128]{1,0:T(8,128)S(1)} custom-call(f32[128,128]{1,0:T(8,128)S(1)} %cholesky.236), custom_call_target="Cholesky" | custom-call | tf_op jit(solution)/shard_map/jit(cholesky)/cholesky | solution.py:213
  336.2 9.8 %custom-call.35 = f32[1,128,128]{1,2,0:T(8,128)S(1)} custom-call(f32[1,128,128]{2,1,0:T(8,128)S(1)} %get-tuple-element.47), custom_call_target="InvertDiagBlocksLowerTriangular" | custom-call | tf_op jit(solution)/shard_map/jit(cholesky)/cholesky | solution.py:213
  346.7 11.9 %cholesky.204 = f32[128,128]{1,0:T(8,128)S(1)} custom-call(f32[128,128]{1,0:T(8,128)S(1)} %cholesky.241), custom_call_target="Cholesky" | custom-call | tf_op jit(solution)/shard_map/jit(cholesky)/cholesky | solution.py:213
  359.3 9.8 %custom-call.36 = f32[1,128,128]{1,2,0:T(8,128)S(1)} custom-call(f32[1,128,128]{2,1,0:T(8,128)S(1)} %get-tuple-element.44), custom_call_target="InvertDiagBlocksLowerTriangular" | custom-call | tf_op jit(solution)/shard_map/jit(cholesky)/cholesky | solution.py:213
  369.7 11.7 %cholesky.221 = f32[128,128]{1,0:T(8,128)S(1)} custom-call(f32[128,128]{1,0:T(8,128)S(1)} %convolution_subtract_fusion.5), custom_call_target="Cholesky" | custom-call | tf_op jit(solution)/shard_map/jit(cholesky)/cholesky | solution.py:213
  384.8 8.0 %while.1 = (s32[]{:T(128)}, f32[512,512]{1,0:T(8,128)S(1)}, s32[4,2]{0,1:T(2,128)S(1)}, f32[4,128,128]{2,1,0:T(8,128)S(1)}, s32[]{:T(128)}) while((s32[]{:T(128)}, f32[512,512]{1,0:T(8,128)S(1)}, s32[4,2]{0,1:T(2,128)S(1)}, f32[4,128,128]{2,1,0:T(8,128)S(1)}, s32[]{:T(128)}) %tuple.64), condition=%wide.while_cond, body=%wide.while_body.sunk | while | flops 2 | bytes 131181 | solution.py:214
  392.8 39.7 %custom-call.37 = f32[4,128,128]{1,2,0:T(8,128)S(1)} custom-call(f32[4,128,128]{2,1,0:T(8,128)S(1)} %get-tuple-element.10), custom_call_target="InvertDiagBlocksLowerTriangular" | custom-call | tf_op jit(solution)/shard_map/jit(_solve_triangular)/triangular_solve | solution.py:214
  432.5 3.8 copy.113
  445.8 4.3 pad_maximum_fusion
  450.0 6.1 %copy.63 = f32[2304,512]{1,0:T(8,128)} copy(f32[2304,512]{0,1:T(8,128)} %get-tuple-element.37) | data formatting | bytes 9437184 | tf_op jit(solution)/shard_map/transpose | solution.py:214
  456.1 7.6 %fusion.2 = f32[8,128,512]{2,0,1:T(8,128)S(1)} fusion(f32[18,128,512]{2,1,0:T(8,128)} %bitcast.264, s32[8]{0:T(128)S(1)} %get-tuple-element.30), kind=kOutput, calls=%fused_computation.6 | convolution fusion | flops 113246352 | bytes 6815776 | tf_op jit(solution)/shard_map/sp,pra->sra/dot_general | solution.py:225
  463.7 5.9 %fusion = f32[8,128,512]{2,0,1:T(8,128)} fusion(f32[18,128,512]{2,1,0:T(8,128)S(1)} %bitcast.266, s32[8]{0:T(128)S(1)} %get-tuple-element.29), kind=kOutput, calls=%fused_computation.4 | convolution fusion | flops 113246352 | bytes 6815776 | tf_op jit(solution)/shard_map/sp,pra->sra/dot_general | solution.py:226
  478.8 6.7 %fusion.28 = f32[8,128,128]{2,1,0:T(8,128)} fusion(f32[8,128,128]{2,1,0:T(8,128)S(1)} %bitcast_add_fusion.2, f32[8,128,512]{2,0,1:T(8,128)} %fusion, f32[8,128,512]{2,0,1:T(8,128)S(1)} %fusion.2, pred[8]{0:T(512)(128)(4,1)S(1)} %get-tuple-element.28), kind=kOutput, calls=%fused_computation.37 | convolution fusion | flops 805568512 | bytes 5242888 | tf_op jit(solution)/shard_map/sra,sca->src/dot_general | solution.py:227
  (150 shorter events, 78.8 us)
Async XLA Ops:
  7.2 108.6 %copy-start = (f32[32,128]{1,0:T(8,128)S(1)}, f32[32,128]{1,0:T(8,128)}, u32[]{:S(2)}) copy-start(f32[32,128]{1,0:T(8,128)} %param.21) | copy-start | bytes 49156
  13.8 2.0 copy-start.17
  15.8 1.4 copy-start.5
  17.2 1.2 copy-start.3
  18.5 3.5 copy-start.9
  27.1 4.4 copy-start.11
  27.1 5.0 %copy-start.15 = (s32[60]{0:T(128)S(1)}, s32[60]{0:T(128)}, u32[]{:S(2)}) copy-start(s32[60]{0:T(128)} %constant.368.clone) | copy-start | bytes 724
  27.1 5.0 %copy-start.16 = (s32[60]{0:T(128)S(1)}, s32[60]{0:T(128)}, u32[]{:S(2)}) copy-start(s32[60]{0:T(128)} %constant.369.clone) | copy-start | bytes 724
  27.1 35.7 %all-to-all-start = ((f32[36,128,128]{2,0,1:T(8,128)}), f32[36,128,128]{2,0,1:T(8,128)S(1)}, u32[]{:S(2)}, u32[]{:S(2)}) async-start(f32[36,128,128]{2,0,1:T(8,128)} %copy.49), calls=%async_computation | async-start | bytes 5242880 | tf_op jit(solution)/shard_map/all_to_all | solution.py:131
  37.1 26.2 %copy-start.10 = (f32[60,144,1]{1,0,2:T(8,128)S(1)}, f32[60,144,1]{1,0,2:T(8,128)}, u32[]{:S(2)}) copy-start(f32[60,144,1]{1,0,2:T(8,128)} %constant.431) | copy-start | bytes 103684
  68.2 40.5 %all-to-all-start.1 = ((f32[88,32,128]{2,1,0:T(8,128)}), f32[88,32,128]{2,1,0:T(8,128)S(1)}, u32[]{:S(2)}, u32[]{:S(2)}) async-start(f32[88,32,128]{2,1,0:T(8,128)} %copy.52), calls=%async_computation.1 | async-start | bytes 2883584 | tf_op jit(solution)/shard_map/all_to_all | solution.py:148
  111.3 12.3 %all-to-all-start.2 = ((f32[32,32,128]{2,1,0:T(8,128)}), f32[32,32,128]{2,1,0:T(8,128)S(1)}, u32[]{:S(2)}, u32[]{:S(2)}) async-start(f32[32,32,128]{2,1,0:T(8,128)} %copy.54), calls=%async_computation.2 | async-start | bytes 1048576 | tf_op jit(solution)/shard_map/all_to_all | solution.py:159
  114.8 156.0 %all-reduce.4.cloned.1.call-start = ((), (), s32[]{:S(2)}) async-start(), calls=%async_computation.3 | async-start | bytes 7864320 | tf_op jit(solution)/shard_map/psum | solution.py:194
  131.1 0.7 copy-start.12
  131.1 1.4 copy-start.4
  131.8 7.1 %copy-start.14 = (s32[72]{0:T(128)S(1)}, s32[72]{0:T(128)}, u32[]{:S(2)}) copy-start(s32[72]{0:T(128)} %constant.430) | copy-start | bytes 868
  131.8 17.4 %copy-start.13 = (f32[1,128]{1,0:T(1,128)S(1)}, f32[1,128]{1,0:T(1,128)}, u32[]{:S(2)}) copy-start(f32[1,128]{1,0:T(1,128)} %param.20) | copy-start | bytes 1540
  136.1 6.7 %collective-permute-start = (f32[128]{0:T(128)S(1)}, f32[128]{0:T(128)S(1)}, u32[]{:S(2)}, u32[]{:S(2)}) collective-permute-start(f32[128]{0:T(128)S(1)} %get-tuple-element.57), channel_id=1, source_target_pairs={{0,1},{1,2},{2,3},{3,4},{4,5},{5,6},{6,7},{7,8},{8,9},{9,10},{10,1... | collective-permute-start | bytes 1544 | tf_op jit(solution)/shard_map/ppermute | solution.py:18
  136.2 7.2 %collective-permute-start.1 = (f32[128]{0:T(128)S(1)}, f32[128]{0:T(128)S(1)}, u32[]{:S(2)}, u32[]{:S(2)}) collective-permute-start(f32[128]{0:T(128)S(1)} %get-tuple-element.63), channel_id=1, source_target_pairs={{0,2},{1,3},{2,4},{3,5},{4,6},{5,7},{6,8},{7,9},{8,10},{9,11},{10,... | collective-permute-start | bytes 1544 | tf_op jit(solution)/shard_map/ppermute | solution.py:18
  136.6 8.8 %collective-permute-start.2 = (f32[128]{0:T(128)S(1)}, f32[128]{0:T(128)S(1)}, u32[]{:S(2)}, u32[]{:S(2)}) collective-permute-start(f32[128]{0:T(128)S(1)} %get-tuple-element.62), channel_id=1, source_target_pairs={{0,3},{1,4},{2,5},{3,6},{4,7},{5,8},{6,9},{7,10},{8,11},{9,12},{10... | collective-permute-start | bytes 1544 | tf_op jit(solution)/shard_map/ppermute | solution.py:18
  138.9 6.5 %collective-permute-start.3 = (f32[128]{0:T(128)S(1)}, f32[128]{0:T(128)S(1)}, u32[]{:S(2)}, u32[]{:S(2)}) collective-permute-start(f32[128]{0:T(128)S(1)} %get-tuple-element.61), channel_id=1, source_target_pairs={{0,4},{1,5},{2,6},{3,7},{4,8},{5,9},{6,10},{7,11},{8,12},{9,13},{1... | collective-permute-start | bytes 1544 | tf_op jit(solution)/shard_map/ppermute | solution.py:18
  138.9 6.5 %collective-permute-start.4 = (f32[128]{0:T(128)S(1)}, f32[128]{0:T(128)S(1)}, u32[]{:S(2)}, u32[]{:S(2)}) collective-permute-start(f32[128]{0:T(128)S(1)} %get-tuple-element.60), channel_id=1, source_target_pairs={{0,5},{1,6},{2,7},{3,8},{4,9},{5,10},{6,11},{7,12},{8,13},{9,14},{... | collective-permute-start | bytes 1544 | tf_op jit(solution)/shard_map/ppermute | solution.py:18
  142.8 6.3 %collective-permute-start.5 = (f32[128]{0:T(128)S(1)}, f32[128]{0:T(128)S(1)}, u32[]{:S(2)}, u32[]{:S(2)}) collective-permute-start(f32[128]{0:T(128)S(1)} %get-tuple-element.59), channel_id=1, source_target_pairs={{0,6},{1,7},{2,8},{3,9},{4,10},{5,11},{6,12},{7,13},{8,14},{9,15},... | collective-permute-start | bytes 1544 | tf_op jit(solution)/shard_map/ppermute | solution.py:18
  143.4 5.7 %collective-permute-start.6 = (f32[128]{0:T(128)S(1)}, f32[128]{0:T(128)S(1)}, u32[]{:S(2)}, u32[]{:S(2)}) collective-permute-start(f32[128]{0:T(128)S(1)} %get-tuple-element.58), channel_id=1, source_target_pairs={{0,7},{1,8},{2,9},{3,10},{4,11},{5,12},{6,13},{7,14},{8,15},{9,16}... | collective-permute-start | bytes 1544 | tf_op jit(solution)/shard_map/ppermute | solution.py:18
  285.0 1.0 copy-start.7
  297.9 24.7 %copy-start.8 = (f32[512,512]{1,0:T(8,128)S(1)}, f32[512,512]{1,0:T(8,128)}, u32[]{:S(2)}) copy-start(f32[512,512]{1,0:T(8,128)} %copy-done.7) | copy-start | bytes 3145732
  392.8 49.6 %copy-start.6 = (f32[512,512]{1,0:T(8,128)}, f32[512,512]{1,0:T(8,128)S(1)}, u32[]{:S(2)}) copy-start(f32[512,512]{1,0:T(8,128)S(1)} %get-tuple-element.133) | copy-start | bytes 3145732
  456.1 7.6 %copy-start.2 = (f32[2304,512]{1,0:T(8,128)S(1)}, f32[2304,512]{1,0:T(8,128)}, u32[]{:S(2)}) copy-start(f32[2304,512]{1,0:T(8,128)} %copy.63) | copy-start | bytes 14155780
  478.8 8.5 %copy-start.1 = (f32[32,128]{1,0:T(8,128)S(1)}, f32[32,128]{1,0:T(8,128)}, u32[]{:S(2)}) copy-start(f32[32,128]{1,0:T(8,128)} %param.21) | copy-start | bytes 49156
Sparse Core Ops, SparseCore 0:
  131.2 139.4 all-reduce.3
where the time goes:
time: 502 us; the launch traced here: 494 us
  waiting for transfers between devices  155 us (31%)
  other arithmetic  134 us (27%)
  local copies, waits for them, and re-layouts  74.4 us (15%)
  matrix products  54.6 us (11%)
  blocking collectives  39 us (8%)
  starting transfers between devices  19.5 us (4%)
  between operations  18 us (4%)
    psum x1, waiting for transfers between devices, per_device(): front_rows, window_rhs = lax.psum((front_rows, window_rhs), ('pts', 'grp'))  82.6 us
    another operation x15, other arithmetic, per_device(): factor = jnp.linalg.cholesky(square)  79.2 us
    another operation x4, other arithmetic, per_device(): panel = jax.scipy.linalg.solve_triangular(factor, columns.T, lower=True).T  44.1 us
    psum x1, blocking collectives, per_device(): front_rows, window_rhs = lax.psum((front_rows, window_rhs), ('pts', 'grp'))  39 us
    all_to_all x1, waiting for transfers between devices, per_device(): lax.all_to_all(outgoing, 'pts', split_axis=0, concat_axis=0, tiled=True)  30.5 us
    all_to_all x1, waiting for transfers between devices, per_device(): lax.all_to_all(band_tiles, 'grp', split_axis=1, concat_axis=0, tiled=True)  25.7 us
    reshape x1, local copies, waits for them, and re-layouts, per_device(): columns = flat_rows[lookup_table].transpose(0, 2, 1, 3).reshape(window_le...  14.8 us
    unnamed x40, local copies, waits for them, and re-layouts  13.1 us
  transfers between devices with their start and end apart: 11, of which 7 were waited for; matrix products, arithmetic and copies ran while one was open for 3% of the time, Pallas kernels for 0%

commit v1 on v0

v1 whole, which is shorter than its diff:
```python
import functools

import jax
import jax.numpy as jnp
from jax import lax
from jax.experimental import pallas as pl
from jax.experimental.pallas import tpu as pltpu
from jax.sharding import PartitionSpec as P

TOUCH = 6
BAND = 8
FRONT = 4
BEFORE = BAND - 1
WINDOW = 2 * BAND - 2 + FRONT
PAIRS = TOUCH * (TOUCH + 1) // 2
GROUP = 8
SPAN = 2 * BAND - 1
AXES = ("pts", "grp")
PRECISE = lax.Precision.HIGHEST
VM = pltpu.VMEM
SM = pltpu.SMEM


def spec(space):
    return pl.BlockSpec(memory_space=space)


def call(kernel, out_shapes, args, spaces, scratch=(), flops=0, nbytes=0):
    return pl.pallas_call(
        kernel,
        out_shape=out_shapes,
        in_specs=[spec(s) for s in spaces],
        out_specs=jax.tree.map(lambda _: spec(VM), out_shapes),
        scratch_shapes=list(scratch),
        cost_estimate=pl.CostEstimate(flops=flops, bytes_accessed=nbytes, transcendentals=0),
        compiler_params=pltpu.CompilerParams(vmem_limit_bytes=56 << 20),
    )(*args)


def nt(a, b, precision=None):
    return lax.dot_general(
        a, b, (((1,), (1,)), ((), ())), precision=precision, preferred_element_type=jnp.float32
    )


def tn(a, b, precision=None):
    return lax.dot_general(
        a, b, (((0,), (0,)), ((), ())), precision=precision, preferred_element_type=jnp.float32
    )


def nn(a, b, precision=None):
    return lax.dot_general(
        a, b, (((1,), (0,)), ((), ())), precision=precision, preferred_element_type=jnp.float32
    )


def pair_index(a, b):
    return (TOUCH - 1) * a - (a * (a - 1)) // 2 + b


def pair_kernel(dims, order, slots, jac, blocks, grad, cam, out, scaled, plain, rhs):
    rows, points, piece, grp_count = dims
    v00, v11, v22 = blocks[0:1, :], blocks[1:2, :], blocks[2:3, :]
    v01, v02, v12 = blocks[3:4, :], blocks[4:5, :], blocks[5:6, :]
    a00 = v11 * v22 - v12 * v12
    a11 = v00 * v22 - v02 * v02
    a22 = v00 * v11 - v01 * v01
    a01 = v02 * v12 - v01 * v22
    a02 = v01 * v12 - v11 * v02
    a12 = v01 * v02 - v00 * v12
    inv = 1.0 / (v00 * a00 + v01 * a01 + v02 * a02)
    vinv = [
        [a00 * inv, a01 * inv, a02 * inv],
        [a01 * inv, a11 * inv, a12 * inv],
        [a02 * inv, a12 * inv, a22 * inv],
    ]
    rhs[...] = jnp.zeros_like(rhs)
    rhs[0:1, :] = cam[...]
    for a in range(TOUCH):
        k = order[a]
        parts = [jac[c, k] for c in range(3)]
        wide = [x.astype(jnp.float32) for x in parts]
        for c in range(3):
            total = wide[0] * vinv[0][c] + wide[1] * vinv[1][c] + wide[2] * vinv[2][c]
            scaled[a, :, c * points : (c + 1) * points] = total.astype(jnp.bfloat16)
            plain[a * rows : (a + 1) * rows, c * points : (c + 1) * points] = parts[c]
    for a in range(TOUCH):
        left = scaled[a]
        pulled = nt(grad[...], left)
        t = slots[a]
        rhs[pl.ds(t, 1), :] = rhs[pl.ds(t, 1), :] - pulled[0:1, :]
        tiles = nt(left, plain[a * rows : TOUCH * rows, :])
        for b in range(a, TOUCH):
            at = pair_index(a, b) * piece
            for e in range(GROUP):
                first = (e % grp_count) * (rows // grp_count) + (e // grp_count) * piece
                out[e, at : at + piece, :] = tiles[
                    first : first + piece, (b - a) * rows : (b - a + 1) * rows
                ]
    for e in range(GROUP):
        out[e, PAIRS * piece : PAIRS * piece + BAND, :] = rhs[...]


def merge_kernel(dims, owner, pick, meta, got, out, rhs):
    piece, pts_count, capacity = dims
    base = meta[0]
    for row in range(SPAN):
        for offset in range(BAND):
            if row + offset >= SPAN:
                continue
            total = None
            for j in range(GROUP):
                t = row - j
                if t < 0 or t + offset > BAND - 1:
                    continue
                at = pick[j * BAND * BAND + t * BAND + offset]
                start = pl.multiple_of(jnp.maximum(at, 0) * piece, piece)
                value = jnp.where(at >= 0, got[j, pl.ds(start, piece), :], 0.0)
                total = value if total is None else total + value
            relative = BAND * row + offset
            dest = owner[lax.rem(base + relative, pts_count)]
            slot = relative // pts_count
            out[dest, slot * piece : (slot + 1) * piece, :] = total
    rhs[...] = jnp.zeros_like(rhs)
    for j in range(GROUP):
        rhs[j : j + BAND, :] = rhs[j : j + BAND, :] + got[j, PAIRS * piece : PAIRS * piece + BAND, :]
    for dest in range(pts_count):
        out[dest, capacity * piece : capacity * piece + 2 * BAND, :] = rhs[...]


def owner_kernel(dims, meta, damping, got, rows_out, direct, mirror, reduced):
    piece, pts_count, capacity, grp_count, quarter, clusters, sets, peers = dims
    residue, my_grp, start = meta[0], meta[1], meta[2]
    halves = GROUP // grp_count
    planes = clusters // GROUP
    cols = rows_out.shape[2]
    offset = lax.rem(residue, BAND)
    part = residue // BAND
    stride = pts_count // BAND
    diag = (
        lax.broadcasted_iota(jnp.int32, (quarter, cols), 0) + my_grp * quarter
        == lax.broadcasted_iota(jnp.int32, (quarter, cols), 1)
    )
    diag = diag & (offset == 0)
    for m in range(BAND * grp_count):
        home = (residue + pts_count * m) // BAND
        plane = home // GROUP
        row = lax.rem(home, GROUP)
        before = lax.rem(plane + planes - 1, planes)
        near = (BAND * row + offset) // pts_count
        far = (BAND * (row + GROUP) + offset) // pts_count
        has_far = row + GROUP + offset < SPAN
        far = jnp.where(has_far, far, 0)
        for y in range(halves):
            value = got[plane * halves + y, pl.ds(pl.multiple_of(near * piece, piece), piece), :]
            extra = got[before * halves + y, pl.ds(pl.multiple_of(far * piece, piece), piece), :]
            rows_out[m, y * piece : (y + 1) * piece, :] = value + jnp.where(has_far, extra, 0.0)
        rows_out[m] = rows_out[m] + jnp.where(diag, damping[pl.ds(home, 1), :], 0.0)
    for i in range(sets):
        j = lax.rem(part + 2 * clusters - start, stride) + stride * i
        home = lax.rem(start + jnp.minimum(j, FRONT - 1), clusters)
        value = rows_out[(BAND * home + offset) // pts_count]
        j = lax.rem(part + 2 * clusters - start + offset, stride) + stride * i
        home = lax.rem(start + jnp.minimum(j, FRONT - 1) + clusters - offset, clusters)
        other = rows_out[(BAND * home + offset) // pts_count]
        for peer in range(peers):
            direct[peer, i * quarter : (i + 1) * quarter, :] = value
            mirror[peer, i * quarter : (i + 1) * quarter, :] = other
    tail = capacity * piece
    for plane in range(planes):
        before = (plane + planes - 1) % planes
        reduced[plane * GROUP : (plane + 1) * GROUP, :] = (
            got[plane * halves, tail : tail + BAND, :]
            + got[before * halves, tail + BAND : tail + 2 * BAND, :]
        )


def fetch(own, other, parity, owner, tile, slot, dims):
    pts_count, grp_count, quarter = dims
    source = owner[lax.rem(tile, pts_count)]
    parts = []
    for g in range(grp_count):
        at = (source * grp_count + g) // 2
        mine = own[at, slot * quarter : (slot + 1) * quarter, :]
        theirs = other[at, slot * quarter : (slot + 1) * quarter, :]
        parts.append(jnp.where(parity == g % 2, mine, theirs))
    return jnp.concatenate(parts, axis=0)


def factor_kernel(dims, meta, owner, own, other, reduced, upper, inverse, behind, work, square):
    pts_count, grp_count, quarter, clusters = dims
    rows = work.shape[0]
    parity, start = meta[3], meta[2]
    stride = pts_count // BAND
    after = BAND - 1
    last = after * rows
    behind[...] = jnp.zeros_like(behind)
    upper[...] = jnp.zeros_like(upper)
    for j in range(FRONT):
        home = lax.rem(start + j, clusters)
        for e in range(BAND):
            tile = fetch(
                own, other, parity, owner, BAND * home + e, j // stride,
                (pts_count, grp_count, quarter),
            )
            if j + e < FRONT:
                if e == 0:
                    tile = 0.5 * (tile + tile.T)
                square[j, :, (j + e) * rows : (j + e + 1) * rows] = tile
            else:
                at = (j + e - FRONT) * rows
                behind[at : at + rows, j * rows : (j + 1) * rows] = tile.T
        behind[last : last + 1, j * rows : (j + 1) * rows] = reduced[pl.ds(home, 1), :]
    row_id = lax.broadcasted_iota(jnp.int32, (rows, 1), 0)
    col_id = lax.broadcasted_iota(jnp.int32, (1, rows), 1)
    eye = (row_id == col_id).astype(jnp.float32)
    for j in range(FRONT):
        work[:, 0:rows] = square[j, :, j * rows : (j + 1) * rows]
        work[:, rows : 2 * rows] = eye

        def step(k, carry):
            left = work[:, 0:rows]
            column = jnp.sum(jnp.where(col_id == k, left, 0.0), axis=1, keepdims=True)
            line = work[pl.ds(k, 1), :]
            pivot = jnp.sum(jnp.where(col_id == k, line[:, 0:rows], 0.0), axis=1, keepdims=True)
            scale = jnp.where(row_id > k, column * (1.0 / pivot), 0.0)
            work[...] = work[...] - scale * line
            return carry

        lax.fori_loop(0, rows, step, 0)
        left = work[:, 0:rows]
        pivots = jnp.sum(jnp.where(row_id == col_id, left, 0.0), axis=1, keepdims=True)
        norm = lax.rsqrt(pivots)
        solve = jnp.where(row_id >= col_id, work[:, rows : 2 * rows], 0.0) * norm
        inverse[j] = solve
        upper[j, :, j * rows : (j + 1) * rows] = jnp.where(row_id <= col_id, left, 0.0) * norm
        if j < FRONT - 1:
            upper[j, :, (j + 1) * rows :] = nn(solve, square[j, :, (j + 1) * rows :], PRECISE)
        for i in range(j + 1, FRONT):
            square[i, :, i * rows :] = square[i, :, i * rows :] - tn(
                upper[j, :, i * rows : (i + 1) * rows], upper[j, :, i * rows :], PRECISE
            )
    substitute(behind, upper, inverse, rows)


def substitute(panel, upper, inverse, rows):
    for j in range(FRONT):
        block = panel[:, j * rows : (j + 1) * rows]
        for k in range(j):
            block = block - nn(
                panel[:, k * rows : (k + 1) * rows],
                upper[k, :, j * rows : (j + 1) * rows],
                PRECISE,
            )
        panel[:, j * rows : (j + 1) * rows] = nt(block, inverse[j], PRECISE)


def update_kernel(
    dims, meta, owner, own, other, reduced, upper, inverse, behind, owned,
    tiles_out, rhs_out, panel_out, ahead, panel,
):
    pts_count, grp_count, quarter, clusters = dims
    rows = tiles_out.shape[1]
    width = FRONT * rows
    residue, my_grp, start, parity, device = meta[0], meta[1], meta[2], meta[3], meta[4]
    stride = pts_count // BAND
    ahead[...] = jnp.zeros_like(ahead)
    for j in range(FRONT):
        for i in range(j, BEFORE):
            e = BEFORE + j - i
            if e > BEFORE:
                continue
            home = lax.rem(start + j + clusters - e, clusters)
            tile = fetch(
                own, other, parity, owner, BAND * home + e, j // stride,
                (pts_count, grp_count, quarter),
            )
            ahead[i * rows : (i + 1) * rows, j * rows : (j + 1) * rows] = tile
    substitute(ahead, upper, inverse, rows)
    first = pl.ds(pl.multiple_of(my_grp * rows, rows), rows)
    for i in range(BEFORE):
        panel[i] = ahead[i * rows : (i + 1) * rows, :]
        panel[BEFORE + FRONT + i] = behind[i * rows : (i + 1) * rows, :]
    panel_out[0 : BEFORE * rows, :] = ahead[:, first]
    for j in range(FRONT):
        at = (BEFORE + j) * rows
        panel_out[at : at + rows, :] = upper[my_grp, :, j * rows : (j + 1) * rows].T
    panel_out[(BEFORE + FRONT) * rows :, :] = behind[0 : BEFORE * rows, first]
    base = start + clusters - BEFORE

    def rest(position):
        return (position < WINDOW) & ((position < BEFORE) | (position >= BEFORE + FRONT))

    for i in range(BAND):
        tile = residue + pts_count * (BAND * my_grp + i)
        home = tile // BAND
        offset = lax.rem(tile, BAND)
        one = lax.rem(home + 2 * clusters - base, clusters)
        two = lax.rem(home + offset + 2 * clusters - base, clusters)
        for g in range(grp_count):
            tiles_out[i, g * quarter : (g + 1) * quarter, :] = owned[g, i]

        @pl.when(rest(one) & rest(two))
        def _():
            tiles_out[i] = tiles_out[i] - nt(panel[one], panel[two], PRECISE)

    position = lax.rem(device + 2 * clusters - base, clusters)
    mine = reduced[pl.ds(device, 1), :]
    rhs_out[...] = mine
    last = BEFORE * rows

    @pl.when(rest(position))
    def _():
        moved = nt(behind[last : last + 8, :], panel[position], PRECISE)
        rhs_out[...] = mine - moved[0:1, :]

    @pl.when((position >= BEFORE) & (position < BEFORE + FRONT))
    def _():
        at = pl.multiple_of((position - BEFORE) * rows, rows)
        rhs_out[...] = behind[last : last + 1, pl.ds(at, rows)]


def per_device(
    jacobian, point_blocks, point_grad, camera_grad, damping, incidence, tile_owner, front_first
):
    pts_count = lax.axis_size("pts")
    grp_count = lax.axis_size("grp")
    clusters = pts_count * grp_count
    my_grp = lax.axis_index("grp")
    my_pts = lax.axis_index("pts")
    device = my_pts * grp_count + my_grp
    rows = jacobian.shape[2]
    points = jacobian.shape[4]
    piece = rows // GROUP
    quarter = rows // grp_count
    capacity = (BAND * (SPAN - 1)) // pts_count + 1
    stride = pts_count // BAND
    sets = -(-FRONT // stride)
    peers = clusters // 2
    f32 = jnp.float32
    groups = [[GROUP * z + e for e in range(GROUP)] for z in range(clusters // GROUP)]
    same = [[2 * i + c for i in range(peers)] for c in range(2)]
    swap = [(i, i ^ 1) for i in range(clusters)]

    def exchange(value, lists):
        return lax.all_to_all(
            value, AXES, split_axis=0, concat_axis=0, tiled=True, axis_index_groups=lists
        )

    slot = jnp.mod(incidence[0] - device, clusters)
    spread = jnp.broadcast_to(jnp.pad(slot, (0, 2))[None, :], (GROUP, BAND))
    member_slots = exchange(spread, groups)[:, :TOUCH]
    rank = jnp.sum(slot[None, :] < slot[:, None], axis=1)
    placed = rank[None, :] == jnp.arange(TOUCH)[:, None]
    order = jnp.sum(jnp.where(placed, jnp.arange(TOUCH)[None, :], 0), axis=1).astype(jnp.int32)
    sorted_slots = jnp.sum(jnp.where(placed, slot[None, :], 0), axis=1).astype(jnp.int32)
    jac = jnp.transpose(jacobian[0], (2, 0, 1, 3))
    grad = jnp.broadcast_to(point_grad.reshape(1, 3 * points), (16, 3 * points))
    block_rows = PAIRS * piece + BAND
    sent = call(
        functools.partial(pair_kernel, (rows, points, piece, grp_count)),
        jax.ShapeDtypeStruct((GROUP, block_rows, rows), f32),
        (order, sorted_slots, jac, point_blocks[0], grad, camera_grad),
        (SM, SM, VM, VM, VM, VM),
        (
            pltpu.VMEM((TOUCH, rows, 3 * points), jnp.bfloat16),
            pltpu.VMEM((TOUCH * rows, 3 * points), jnp.bfloat16),
            pltpu.VMEM((BAND, rows), f32),
        ),
        flops=2 * PAIRS * rows * rows * 3 * points,
        nbytes=4 * GROUP * block_rows * rows,
    )
    got = exchange(sent, groups)

    here = member_slots[:, None, :] == jnp.arange(BAND)[None, :, None]
    present = jnp.any(here, axis=2)
    less = jnp.sum(
        (member_slots[:, None, :] < jnp.arange(BAND)[None, :, None]).astype(jnp.int32), axis=2
    )
    later = jnp.arange(BAND)[:, None] + jnp.arange(BAND)[None, :]
    at_later = later[:, :, None] == jnp.arange(BAND)[None, None, :]
    less_later = jnp.sum(jnp.where(at_later[None], less[:, None, None, :], 0), axis=3)
    present_later = jnp.any(at_later[None] & present[:, None, None, :], axis=3)
    pick = jnp.where(
        present[:, :, None] & present_later, pair_index(less[:, :, None], less_later), -1
    )
    pick = pick.reshape(GROUP * BAND * BAND).astype(jnp.int32)
    residue = jnp.sum(jnp.arange(pts_count) * (tile_owner == my_pts))
    group_base = jnp.mod((device // GROUP) * GROUP * BAND, pts_count)
    send_rows = capacity * piece + 2 * BAND
    sent = call(
        functools.partial(merge_kernel, (piece, pts_count, capacity)),
        jax.ShapeDtypeStruct((pts_count, send_rows, rows), f32),
        (tile_owner, pick, group_base[None].astype(jnp.int32), got),
        (SM, SM, SM, VM),
        (pltpu.VMEM((2 * BAND, rows), f32),),
        nbytes=4 * (pts_count * send_rows + GROUP * block_rows) * rows,
    )
    got = lax.all_to_all(sent, "pts", split_axis=0, concat_axis=0, tiled=True)

    lane = jnp.arange(8)
    meta = jnp.where(lane == 0, residue, 0)
    meta = jnp.where(lane == 1, my_grp, meta)
    meta = jnp.where(lane == 2, front_first[0], meta)
    meta = jnp.where(lane == 3, jnp.mod(device, 2), meta)
    meta = jnp.where(lane == 4, device, meta).astype(jnp.int32)
    owner_rows, direct, mirror, reduced = call(
        functools.partial(
            owner_kernel,
            (piece, pts_count, capacity, grp_count, quarter, clusters, sets, peers),
        ),
        (
            jax.ShapeDtypeStruct((BAND * grp_count, quarter, rows), f32),
            jax.ShapeDtypeStruct((peers, sets * quarter, rows), f32),
            jax.ShapeDtypeStruct((peers, sets * quarter, rows), f32),
            jax.ShapeDtypeStruct((clusters, rows), f32),
        ),
        (meta, damping, got),
        (SM, VM, VM),
        nbytes=4 * (pts_count * send_rows + 2 * peers * sets * quarter) * rows,
    )
    direct = exchange(direct, same)
    direct_other = lax.ppermute(direct, AXES, swap)
    mirror = exchange(mirror, same)
    mirror_other = lax.ppermute(mirror, AXES, swap)
    owned = lax.all_to_all(owner_rows, "grp", split_axis=0, concat_axis=0, tiled=True)
    owned = owned.reshape(grp_count, BAND, quarter, rows)

    width = FRONT * rows
    dims = (pts_count, grp_count, quarter, clusters)
    upper, inverse, behind = call(
        functools.partial(factor_kernel, dims),
        (
            jax.ShapeDtypeStruct((FRONT, rows, width), f32),
            jax.ShapeDtypeStruct((FRONT, rows, rows), f32),
            jax.ShapeDtypeStruct((BEFORE * rows + 8, width), f32),
        ),
        (meta, tile_owner, direct, direct_other, reduced),
        (SM, SM, VM, VM, VM),
        (
            pltpu.VMEM((rows, 2 * rows), f32),
            pltpu.VMEM((FRONT, rows, width), f32),
        ),
        flops=400 * rows * rows * rows * 6,
        nbytes=8 * peers * sets * quarter * rows,
    )
    tiles_out, rhs_out, front_panel = call(
        functools.partial(update_kernel, dims),
        (
            jax.ShapeDtypeStruct((BAND, rows, rows), f32),
            jax.ShapeDtypeStruct((1, rows), f32),
            jax.ShapeDtypeStruct((WINDOW * rows, rows), f32),
        ),
        (meta, tile_owner, mirror, mirror_other, reduced, upper, inverse, behind, owned),
        (SM, SM, VM, VM, VM, VM, VM, VM, VM),
        (
            pltpu.VMEM((BEFORE * rows, width), f32),
            pltpu.VMEM((WINDOW, rows, width), f32),
        ),
        flops=200 * rows * rows * rows * 6,
        nbytes=8 * peers * sets * quarter * rows,
    )
    return (tiles_out, rhs_out, front_panel)


def solution(mesh):
    in_specs = (
        P(AXES, None, None, None, None),
        P(AXES, None, None),
        P(AXES, None, None),
        P(AXES, None),
        P(),
        P(AXES, None),
        P(),
        P(),
    )
    out_specs = (P(AXES, None, None), P(AXES, None), P(None, "grp"))
    return jax.shard_map(
        per_device, mesh=mesh, in_specs=in_specs, out_specs=out_specs, check_vma=False
    )
```

time: 502 us -> 225 us (0.45); the launches traced: 494 us -> 223 us
  other arithmetic: 134 us -> 6.74 us
  waiting for transfers between devices: 155 us -> 60.8 us
  Pallas kernels: 0 us -> 92.5 us
  local copies, waits for them, and re-layouts: 74.4 us -> 7.83 us
  matrix products: 54.6 us -> 0 us
  between operations: 18 us -> 1.41 us
  blocking collectives: 39 us -> 32.3 us
    another operation x22 -> x0, other arithmetic: 125 us -> none  [the longest x15 79.2 us: per_device(): factor = jnp.linalg.cholesky(square)]
    pallas_call x0 -> x5, Pallas kernels: none -> 92.5 us  [call(): pl.pallas_call(kernel, out_shape=out_shapes, in_specs=[spec(s) for s in s...]
    psum x1 -> x0, waiting for transfers between devices: 82.6 us -> none  [per_device(): front_rows, window_rhs = lax.psum((front_rows, window_rhs), ('pts', 'grp'))]
    dot_general x14 -> x0, matrix products: 39.3 us -> none  [the longest x1 7.63 us: per_device(): jnp.einsum('sp,pra->sra', pick_home, panel_blocks, precision=PRECISE)]
    psum x1 -> x0, blocking collectives: 39 us -> none  [per_device(): front_rows, window_rhs = lax.psum((front_rows, window_rhs), ('pts', 'grp'))]
    all_to_all x0 -> x1, blocking collectives: none -> 32.3 us  [exchange(): lax.all_to_all(value, AXES, split_axis=0, concat_axis=0, tiled=True, axis...]
    another operation x20 -> x0, matrix products: 15.3 us -> none  [the longest x7 9.33 us: per_device(): panel = jax.scipy.linalg.solve_triangular(factor, columns.T, lower=True).T]
    reshape x1 -> x0, local copies, waits for them, and re-layouts: 14.8 us -> none  [per_device(): columns = flat_rows[lookup_table].transpose(0, 2, 1, 3).reshape(window_le...]
  transfers between devices with their start and end apart: 11 -> 7, of which waited for: 7 -> 3; matrix products, arithmetic and copies ran while one was open for 3% -> 5% of each run, Pallas kernels for 0% -> 33%
where the time goes in v1:
time: 225 us; the launch traced here: 223 us
  Pallas kernels  92.5 us (41%)
  waiting for transfers between devices  60.8 us (27%)
  blocking collectives  32.3 us (14%)
  starting transfers between devices  21.9 us (10%)
  local copies, waits for them, and re-layouts  7.83 us (3%)
  other arithmetic  6.74 us (3%)
    pallas_call x5, Pallas kernels, call(): pl.pallas_call(kernel, out_shape=out_shapes, in_specs=[spec(s) for s in s...  92.5 us
    all_to_all x3, waiting for transfers between devices, exchange(): lax.all_to_all(value, AXES, split_axis=0, concat_axis=0, tiled=True, axis...  39.4 us
    all_to_all x1, blocking collectives, exchange(): lax.all_to_all(value, AXES, split_axis=0, concat_axis=0, tiled=True, axis...  32.3 us
    all_to_all x1, waiting for transfers between devices, per_device(): got = lax.all_to_all(sent, 'pts', split_axis=0, concat_axis=0, tiled=True)  21.4 us
    all_to_all x3, starting transfers between devices, exchange(): lax.all_to_all(value, AXES, split_axis=0, concat_axis=0, tiled=True, axis...  13.3 us
    unnamed x18, local copies, waits for them, and re-layouts  5.85 us
    all_to_all x1, starting transfers between devices, per_device(): got = lax.all_to_all(sent, 'pts', split_axis=0, concat_axis=0, tiled=True)  5.01 us
  transfers between devices with their start and end apart: 7, of which 3 were waited for; matrix products, arithmetic and copies ran while one was open for 5% of the time, Pallas kernels for 33%

profile of v1, /device:TPU:0, one launch (start us, length us, event | category | flops | bytes accessed | tf_op | source)
XLA Modules:
  0.0 223.5 jit_solution(12039733585099495169)
XLA Ops:
  0.7 0.7 and_select_fusion.1
  1.3 0.6 broadcast_in_dim.98
  1.9 5.2 %all-to-all-start = ((s32[8,1,8]{2,1,0:T(1,128)}), s32[8,1,8]{2,1,0:T(1,128)S(1)}, u32[]{:S(2)}, u32[]{:S(2)}) async-start(s32[8,1,8]{2,1,0:T(1,128)} %broadcast_in_dim.98), calls=%async_computation | async-start | bytes 8192 | tf_op jit(solution)/shard_map/all_to_all | solution.py:347
  7.1 0.7 fusion.5
  7.8 0.2 convert_reduce_fusion.1
  8.0 0.7 select_reduce_fusion.1
  8.7 2.4 %copy.18 = bf16[1,6,128,3,256]{4,2,1,3,0:T(8,128)(2,1)} copy(bf16[1,6,128,3,256]{4,2,3,1,0:T(8,128)(2,1)} %param.8) | data formatting | bytes 2359296 | tf_op args[0]
  11.1 0.6 copy.19
  11.7 0.6 broadcast_in_dim.106.grad
  12.3 4.1 %shard_map.103 = f32[8,344,128]{2,1,0:T(8,128)} custom-call(s32[6]{0:T(128)} %get-tuple-element.18.order, s32[6]{0:T(128)} %get-tuple-element.17.slots, bf16[3,6,128,256]{3,2,1,0:T(8,128)(2,1)} %bitcast.18, f32[6,256]{1,0:T(8,128)} %bitcast.20, bf16[16,768]{1,0:T(8,128)(2,1)} %broadcast_in_dim.106.grad, f32[1,128]{1,0:T(1,128)} %cam.1), custom_call_target="tpu_custom_call" | custom-call | flops 528482304 | bytes 1409024 | tf_op jit(solution)/shard_map/pallas_call | solution.py:29
  16.4 4.2 %all-to-all-start.1 = ((f32[8,344,128]{2,1,0:T(8,128)}), f32[8,344,128]{2,1,0:T(8,128)S(1)}, u32[]{:S(2)}, u32[]{:S(2)}) async-start(f32[8,344,128]{2,1,0:T(8,128)} %shard_map.103), calls=%async_computation.1 | async-start | bytes 2818048 | tf_op jit(solution)/shard_map/all_to_all | solution.py:347
  20.7 0.1 copy.13
  21.0 1.2 and_reduce_fusion
  22.1 1.2 select_reduce_fusion
  23.3 0.1 add_select_fusion
  23.4 0.7 select_n.84.pick
  24.1 15.8 %all-to-all-done.1.got = f32[8,344,128]{2,1,0:T(8,128)S(1)} async-done(((f32[8,344,128]{2,1,0:T(8,128)}), f32[8,344,128]{2,1,0:T(8,128)S(1)}, u32[]{:S(2)}, u32[]{:S(2)}) %all-to-all-start.1) | async-done | bytes 1409056 | tf_op jit(solution)/shard_map/all_to_all | solution.py:347
  39.9 1.1 copy-done
  41.0 3.2 %shard_map.104 = f32[8,256,128]{2,1,0:T(8,128)} custom-call(s32[8]{0:T(128)} %owner.5, s32[512]{0:T(512)} %select_n.84.pick, s32[1]{0:T(128)} %bitcast.3.meta, f32[8,344,128]{2,1,0:T(8,128)} %copy-done), custom_call_target="tpu_custom_call" | custom-call | bytes 2457600 | tf_op jit(solution)/shard_map/pallas_call | solution.py:29
  44.2 5.0 %all-to-all-start.2 = ((f32[8,256,128]{2,1,0:T(8,128)}), f32[8,256,128]{2,1,0:T(8,128)S(1)}, u32[]{:S(2)}, u32[]{:S(2)}) async-start(f32[8,256,128]{2,1,0:T(8,128)} %shard_map.104), calls=%async_computation.2 | async-start | bytes 2097152 | tf_op jit(solution)/shard_map/all_to_all | solution.py:400
  49.9 0.6 fusion.4
  50.5 1.2 compare_select_fusion.9.meta
  51.7 21.4 %all-to-all-done.2.got = f32[8,256,128]{2,1,0:T(8,128)S(1)} async-done(((f32[8,256,128]{2,1,0:T(8,128)}), f32[8,256,128]{2,1,0:T(8,128)S(1)}, u32[]{:S(2)}, u32[]{:S(2)}) %all-to-all-start.2) | async-done | bytes 1048608 | tf_op jit(solution)/shard_map/all_to_all | solution.py:400
  73.1 1.0 copy-done.1
  74.1 3.6 %shard_map.105 = (f32[32,32,128]{2,1,0:T(8,128)}, f32[16,128,128]{2,1,0:T(8,128)}, f32[16,128,128]{2,1,0:T(8,128)}, f32[32,128]{1,0:T(8,128)}) custom-call(s32[8]{0:T(128)} %compare_select_fusion.9.meta, f32[32,128]{1,0:T(8,128)} %damping.1, f32[8,256,128]{2,1,0:T(8,128)} %copy-done.1), custom_call_target="tpu_custom_call" | custom-call | bytes 3145728 | tf_op jit(solution)/shard_map/pallas_call | solution.py:29
  77.7 32.3 %all_to_all.34.own = f32[16,128,128]{2,1,0:T(8,128)S(1)} all-to-all(f32[16,128,128]{2,1,0:T(8,128)} %get-tuple-element.12), channel_id=1, replica_groups={{0,2,4,6,8,10,12,14,16,18,20,22,24,26,28,30},{1,3,5,7,9,11,13,15,17,19,..., dimensions={0} | all-to-all | bytes 2097152 | tf_op jit(solution)/shard_map/all_to_all | solution.py:347
  110.0 3.9 %all-to-all-start.3 = ((f32[16,128,128]{2,1,0:T(8,128)}), f32[16,128,128]{2,1,0:T(8,128)S(1)}, u32[]{:S(2)}, u32[]{:S(2)}) async-start(f32[16,128,128]{2,1,0:T(8,128)} %get-tuple-element.10), calls=%async_computation.3 | async-start | bytes 2097152 | tf_op jit(solution)/shard_map/all_to_all | solution.py:347
  114.0 23.6 %all-to-all-done.3.own = f32[16,128,128]{2,1,0:T(8,128)S(1)} async-done(((f32[16,128,128]{2,1,0:T(8,128)}), f32[16,128,128]{2,1,0:T(8,128)S(1)}, u32[]{:S(2)}, u32[]{:S(2)}) %all-to-all-start.3) | async-done | bytes 1048608 | tf_op jit(solution)/shard_map/all_to_all | solution.py:347
  137.6 3.5 %all-to-all-start.5 = ((f32[32,32,128]{2,1,0:T(8,128)}), f32[32,32,128]{2,1,0:T(8,128)S(1)}, u32[]{:S(2)}, u32[]{:S(2)}) async-start(f32[32,32,128]{2,1,0:T(8,128)} %get-tuple-element.16), calls=%async_computation.5 | async-start | bytes 1048576 | tf_op jit(solution)/shard_map/all_to_all | solution.py:427
  141.1 70.5 %shard_map.106 = (f32[4,128,512]{2,1,0:T(8,128)}, f32[4,128,128]{2,1,0:T(8,128)}, f32[904,512]{1,0:T(8,128)}) custom-call(s32[8]{0:T(128)} %compare_select_fusion.9.meta, s32[8]{0:T(128)} %owner.5, f32[16,128,128]{2,1,0:T(8,128)} %copy-done.3, f32[16,128,128]{2,1,0:T(8,128)} %collective-permute-done.1.other, f32[32,128]{1,0:T(8,128)} %get-tuple-element.11.reduced), custom_call_target="tpu_custom_call" | custom-call | flops 5033164800 | bytes 2097152 | tf_op jit(solution)/shard_map/pallas_call | solution.py:29
  211.6 0.8 copy-done.4
  212.4 11.0 %shard_map.107 = (f32[8,128,128]{2,1,0:T(8,128)}, f32[1,128]{1,0:T(1,128)}, f32[2304,128]{1,0:T(8,128)}) custom-call(s32[8]{0:T(128)} %compare_select_fusion.9.meta, s32[8]{0:T(128)} %owner.5, f32[16,128,128]{2,1,0:T(8,128)} %copy-done.2, f32[16,128,128]{2,1,0:T(8,128)} %collective-permute-done.other, f32[32,128]{1,0:T(8,128)} %get-tuple-element.11.reduced, ...), custom_call_target="tpu_custom_call" | custom-call | flops 2516582400 | bytes 2097152 | tf_op jit(solution)/shard_map/pallas_call | solution.py:29
  (26 shorter events, 0.4 us)
Async XLA Ops:
  0.6 10.4 %copy-start.6 = (bf16[1,3,256]{2,1,0:T(4,128)(2,1)S(1)}, bf16[1,3,256]{2,1,0:T(4,128)(2,1)}, u32[]{:S(2)}) copy-start(bf16[1,3,256]{2,1,0:T(4,128)(2,1)} %param.10) | copy-start | bytes 4612
  0.6 10.4 %copy-start.5 = (f32[1,6,256]{2,0,1:T(1,128)S(1)}, f32[1,6,256]{2,0,1:T(1,128)}, u32[]{:S(2)}) copy-start(f32[1,6,256]{2,0,1:T(1,128)} %param.9) | copy-start | bytes 18436
  1.9 14.5 %all-to-all-start = ((s32[8,1,8]{2,1,0:T(1,128)}), s32[8,1,8]{2,1,0:T(1,128)S(1)}, u32[]{:S(2)}, u32[]{:S(2)}) async-start(s32[8,1,8]{2,1,0:T(1,128)} %broadcast_in_dim.98), calls=%async_computation | async-start | bytes 8192 | tf_op jit(solution)/shard_map/all_to_all | solution.py:347
  16.4 23.4 %all-to-all-start.1 = ((f32[8,344,128]{2,1,0:T(8,128)}), f32[8,344,128]{2,1,0:T(8,128)S(1)}, u32[]{:S(2)}, u32[]{:S(2)}) async-start(f32[8,344,128]{2,1,0:T(8,128)} %shard_map.103), calls=%async_computation.1 | async-start | bytes 2818048 | tf_op jit(solution)/shard_map/all_to_all | solution.py:347
  39.9 1.1 copy-start
  44.2 5.7 %copy-start.7 = (s32[8]{0:T(128)S(1)}, s32[8]{0:T(128)}, u32[]{:S(2)}) copy-start(s32[8]{0:T(128)} %owner.5) | copy-start | bytes 100
  44.2 28.9 %all-to-all-start.2 = ((f32[8,256,128]{2,1,0:T(8,128)}), f32[8,256,128]{2,1,0:T(8,128)S(1)}, u32[]{:S(2)}, u32[]{:S(2)}) async-start(f32[8,256,128]{2,1,0:T(8,128)} %shard_map.104), calls=%async_computation.2 | async-start | bytes 2097152 | tf_op jit(solution)/shard_map/all_to_all | solution.py:400
  73.1 1.0 copy-start.1
  110.0 27.6 %copy-start.3 = (f32[16,128,128]{2,1,0:T(8,128)}, f32[16,128,128]{2,1,0:T(8,128)S(1)}, u32[]{:S(2)}) copy-start(f32[16,128,128]{2,1,0:T(8,128)S(1)} %all_to_all.34.own) | copy-start | bytes 3145732
  110.0 27.6 %all-to-all-start.3 = ((f32[16,128,128]{2,1,0:T(8,128)}), f32[16,128,128]{2,1,0:T(8,128)S(1)}, u32[]{:S(2)}, u32[]{:S(2)}) async-start(f32[16,128,128]{2,1,0:T(8,128)} %get-tuple-element.10), calls=%async_computation.3 | async-start | bytes 2097152 | tf_op jit(solution)/shard_map/all_to_all | solution.py:347
  113.9 27.2 %collective-permute-start.1 = (f32[16,128,128]{2,1,0:T(8,128)S(1)}, f32[16,128,128]{2,1,0:T(8,128)}, u32[]{:S(2)}, u32[]{:S(2)}) collective-permute-start(f32[16,128,128]{2,1,0:T(8,128)S(1)} %all_to_all.34.own), channel_id=1, source_target_pairs={{0,1},{1,0},{2,3},{3,2},{4,5},{5,4},{6,7},{7,6},{8,9},{9,8},{10,11... | collective-permute-start | bytes 3145736 | tf_op jit(solution)/shard_map/ppermute | solution.py:424
  137.6 74.0 %copy-start.2 = (f32[16,128,128]{2,1,0:T(8,128)}, f32[16,128,128]{2,1,0:T(8,128)S(1)}, u32[]{:S(2)}) copy-start(f32[16,128,128]{2,1,0:T(8,128)S(1)} %all-to-all-done.3.own) | copy-start | bytes 3145732
  137.6 74.0 %collective-permute-start = (f32[16,128,128]{2,1,0:T(8,128)S(1)}, f32[16,128,128]{2,1,0:T(8,128)}, u32[]{:S(2)}, u32[]{:S(2)}) collective-permute-start(f32[16,128,128]{2,1,0:T(8,128)S(1)} %all-to-all-done.3.own), channel_id=1, source_target_pairs={{0,1},{1,0},{2,3},{3,2},{4,5},{5,4},{6,7},{7,6},{8,9},{9,8},{10,11... | collective-permute-start | bytes 3145736 | tf_op jit(solution)/shard_map/ppermute | solution.py:426
  137.6 74.0 %all-to-all-start.5 = ((f32[32,32,128]{2,1,0:T(8,128)}), f32[32,32,128]{2,1,0:T(8,128)S(1)}, u32[]{:S(2)}, u32[]{:S(2)}) async-start(f32[32,32,128]{2,1,0:T(8,128)} %get-tuple-element.16), calls=%async_computation.5 | async-start | bytes 1048576 | tf_op jit(solution)/shard_map/all_to_all | solution.py:427
  211.6 0.8 copy-start.4
